TPU v7x, 32 devices: a whole 2x2x4 slice. The times are simulated.
32 devices in a mesh: vox: 32 (over z, y, x, core).
Axes of the slice: x: 2, y: 2, z: 4, core: 2. Of those that a mesh axis runs over, the one named last changes fastest.
Arguments:
- voxels: bfloat16 [32768, 512], P('vox'), may hold values from -6 to 6
- hilbert_rank: int32 [32768], P('vox'), may hold values from 0 to 32767, as said below
- z_rank: int32 [32768], P('vox'), may hold values from 0 to 32767, as said below
- parent_slot: int32 [4096], P('vox'), may hold values from 0 to 4095, as said below
- qkv_weight: bfloat16 [2, 512, 1536], replicated, as said below
- out_weight: bfloat16 [2, 512, 512], replicated, may hold values from -0.25 to 0.25
- up_weight: bfloat16 [2, 512, 2048], replicated, may hold values from -0.25 to 0.25
- down_weight: bfloat16 [2, 2048, 512], replicated, may hold values from -0.125 to 0.125
- norm_gains: float32 [2, 2, 512], replicated, may hold values from 0.25 to 1.75
Outputs:
- pooled: float32 [4096, 512], P('vox')
Inputs may be any that keep to these rules, and one draw needn't show every extreme that they name: `hilbert_rank`: A permutation. The 1024 voxels of one device have at most 64 Hilbert positions in any one range of 1024 consecutive positions; such counts take only the values 0, 32 and 64, and 64 is reached. `z_rank`: A permutation. The voxels whose Hilbert positions lie in one range of 1024 consecutive positions have at most 64 z ranks in any one such range; counts take only the values 0, 32 and 64, and 64 is reached. `parent_slot`: A permutation. The 128 parents of one range of consecutive parent numbers have at most 8 slots in any one range of 128 consecutive slots; counts take only the values 0, 4 and 8, and 8 is reached. `qkv_weight`: entries of order 512 ** -0.5 times a factor of at most 7.
All inputs are finite; a program needn't handle non-finite values.
Results may differ from a plain program's by a relative error of at most 0.0085.
Values may be sent and summed in bfloat16 or wider, within the bound.
No kernel may reach another device: no remote copies, remote signals or barrier semaphores. Data moves between devices by JAX's collectives and lax.ppermute only.
A program may use at most 128 MiB of HBM per device.

v0:
```python
import functools

import jax
import jax.numpy as jnp
from jax import lax
from jax.experimental import pallas as pl
from jax.experimental.pallas import tpu as pltpu
from jax.sharding import PartitionSpec as P

HEADS = 8
LANES = 128
SUB = 8
GROUP = 8
TILE = 256
PART = 16
LABEL_ROW = 7
F32 = jnp.float32
BF16 = jnp.bfloat16
I32 = jnp.int32
LOG2E = 1.4426950408889634
GELU_C = 0.7978845608028654
ONES = 16
NT = (((1,), (1,)), ((), ()))


def dot(a, b, dims=(((1,), (0,)), ((), ()))):
    return lax.dot_general(a, b, dims, preferred_element_type=F32)


def iota(shape, axis):
    return lax.broadcasted_iota(I32, shape, axis)


def one_hot(mask):
    return mask.astype(F32).astype(BF16)


def log2(value):
    bits = value.bit_length() - 1
    assert 1 << bits == value
    return bits


def tile_at(t):
    return pl.ds(t * TILE if isinstance(t, int) else pl.multiple_of(t * TILE, TILE), TILE)


def lane_cuts(size):
    return range(0, size, LANES)


def rank_rows(dest, n_dev):
    tri = (iota((LANES, LANES), 0) <= iota((LANES, LANES), 1)).astype(F32)
    tri = jnp.concatenate([tri, jnp.ones((LANES, LANES), F32)], axis=1).astype(BF16)
    dev = iota((n_dev, LANES), 0)
    seen = jnp.zeros((n_dev, LANES), F32)
    chunks = []
    for at in lane_cuts(dest.shape[1]):
        hot = (dest[:, at : at + LANES] == dev).astype(F32)
        both = dot(hot.astype(BF16), tri)
        chunks.append((hot, both[:, :LANES] + seen))
        seen = seen + both[:, LANES:]
    return chunks, seen


def pick(hot, table):
    return jnp.sum(hot * table, axis=0, keepdims=True)


def part_starts(counts, parts):
    n_dev = counts.shape[0]
    below = one_hot(iota((n_dev, n_dev), 1) < iota((n_dev, n_dev), 0))
    return dot(below, counts.astype(BF16)) * (1.0 / parts)


def sort_places(dest, n_dev, rows, parts):
    chunks, counts = rank_rows(dest, n_dev)
    starts = part_starts(counts, parts)
    part_rows = rows // parts
    cap = parts * PART
    places = []
    for hot, run in chunks:
        order = pick(hot, run - 1).astype(I32)
        count = pick(hot, counts).astype(I32)
        start = pick(hot, starts).astype(I32)
        full = count == cap
        part = jnp.where(full, order >> log2(PART), order >> log2(PART // 2))
        inside = order - part * jnp.where(full, PART, PART // 2)
        places.append(jnp.where(count > 0, part * part_rows + start + inside, -1))
    return jnp.concatenate(places, axis=1), counts, starts


def part_slots(counts, starts, part_rows, parts):
    n_dev = counts.shape[0]
    share = counts * (1.0 / parts)
    dev = iota((n_dev, LANES), 0).astype(F32) * PART
    slots = []
    for at in lane_cuts(part_rows):
        k = (iota((n_dev, LANES), 1) + at).astype(F32)
        inside = ((k >= starts) & (k < starts + share)).astype(F32)
        slots.append(pick(inside, dev + k - starts))
    return jnp.concatenate(slots, axis=1).astype(I32)


def group_slots(parent, n_dev, stride):
    chunks, _ = rank_rows(parent >> log2(parent.shape[1]), n_dev)
    dev = iota((n_dev, LANES), 0).astype(F32) * stride
    return jnp.concatenate([pick(hot, run - 1 + dev) for hot, run in chunks], axis=1).astype(I32)


def emit_rows(slot_row, rows, meta, group, out_ref, ids_ref):
    span = (out_ref.shape[1] - SUB) // (rows.shape[1] // LANES)
    for t in range(ids_ref.shape[1] // TILE):
        hot = one_hot(slot_row - t * TILE == iota((TILE, slot_row.shape[1]), 0))
        placed = dot(hot, rows).astype(BF16)
        ids_ref[:, tile_at(t)] += dot(meta, hot, NT)
        for d in range(TILE // PART):
            for c in range(rows.shape[1] // LANES):
                at = c * span + group * PART
                out_ref[t * (TILE // PART) + d, at : at + PART, :] = placed[
                    d * PART : (d + 1) * PART, c * LANES : (c + 1) * LANES
                ]


def emit_ids(me, out_ref, ids_ref):
    per_tile = LANES // PART
    mine = lax.rem(me, per_tile)
    owned = iota((SUB, LANES), 1) // PART == mine
    at = out_ref.shape[1] - SUB
    for dev in range(out_ref.shape[0]):
        cut = dev // per_tile * LANES
        turn = lax.rem(mine + (per_tile - dev % per_tile), per_tile) * PART
        part = pltpu.roll(ids_ref[:, cut : cut + LANES], turn, 1)
        out_ref[dev, at:, :] = jnp.where(owned, part, 0.0).astype(BF16)


def slot_ids(got_ref):
    n_dev, depth, _ = got_ref.shape
    per_tile = LANES // PART
    tiles = []
    for first in range(0, n_dev, per_tile):
        total = got_ref[first, depth - SUB :, :].astype(F32)
        for j in range(1, per_tile):
            total = total + got_ref[first + j, depth - SUB :, :].astype(F32)
        tiles.append(total)
    return jnp.concatenate(tiles, axis=1)


def slot_rows(got_ref, group, lanes_of):
    n_dev, depth, _ = got_ref.shape
    span = (depth - SUB) // lanes_of
    return jnp.concatenate(
        [
            got_ref[:, c * span + group * PART : c * span + (group + 1) * PART, :].reshape(n_dev * PART, LANES)
            for c in range(lanes_of)
        ],
        axis=1,
    )


def layer_norm(stream, gain_row):
    row_mean = jnp.mean(stream, axis=-1, keepdims=True)
    centred = stream - row_mean
    row_var = jnp.mean(centred * centred, axis=-1, keepdims=True)
    return centred * lax.rsqrt(row_var + 1e-05) * gain_row


def gelu(x):
    inner = x * (x * x * (0.044715 * GELU_C) + GELU_C)
    half = 0.5 * x
    return half + half * jnp.tanh(inner)


def project_tile(t, x_ref, qk_ref, vt_ref, qkv_w, gains):
    width = x_ref.shape[1]
    head = width // HEADS
    at = tile_at(t)
    normed = layer_norm(x_ref[at, :].astype(F32), gains[0:1, :]).astype(BF16)
    qk_ref[at, :width] = (dot(normed, qkv_w[:, :width]) * (LOG2E * head**-0.5)).astype(BF16)
    qk_ref[at, width:] = dot(normed, qkv_w[:, width : 2 * width]).astype(BF16)
    values = dot(normed, qkv_w[:, 2 * width :]).T.astype(BF16)
    for h in range(HEADS):
        vt_ref[h, :head, at] = values[h * head : (h + 1) * head, :]


def fill_ones(vt_ref):
    depth = vt_ref.shape[1]
    for h in range(HEADS):
        vt_ref[h, depth - ONES :, :] = jnp.ones((ONES, vt_ref.shape[2]), BF16)


def run_tiles(low, high, x_ref, y_ref, state, weights, gains):
    qk_ref, vt_ref, att_ref, mid_ref, sum_ref, score_ref = state
    _, out_w, up_w, down_w = weights
    rows, width = x_ref.shape
    head = width // HEADS
    pairs = width // LANES
    per_pair = LANES // head
    piece = up_w.shape[1] // pairs
    owner = iota((TILE, LANES), 1) // head
    cuts = [slice(at, at + TILE) for at in range(0, rows, TILE)]

    def masked_queries(t, pair):
        queries = qk_ref[tile_at(t), pair * LANES : (pair + 1) * LANES]
        return [jnp.where(owner == j, queries, jnp.zeros_like(queries)) for j in range(per_pair)]

    def score_cut(own, pair, cut, tops):
        key_rows = qk_ref[cut, width + pair * LANES : width + (pair + 1) * LANES]
        result = []
        for j in range(per_pair):
            scores = dot(key_rows, own[j], NT)
            score_ref[pair % 2, j, cut, :] = scores
            top = jnp.max(scores.reshape(TILE // SUB, SUB, TILE), axis=0)
            result.append(top if tops is None else jnp.maximum(tops[j], top))
        return result

    def mix_cut(pair, cut, tops, sums):
        result = []
        for j in range(per_pair):
            probs = jnp.exp2(score_ref[pair % 2, j, cut, :] - tops[j]).astype(BF16)
            mixed = dot(vt_ref[pair * per_pair + j, :, cut], probs)
            result.append(mixed if sums is None else sums[j] + mixed)
        return result

    def attend_pair(pair, tops, next_tile):
        after = (pair + 1) % pairs
        own = None if next_tile is None else masked_queries(next_tile, after)
        tops = [jnp.max(top, axis=0, keepdims=True) for top in tops]
        next_tops, sums = None, None
        for cut in cuts:
            if own is not None:
                next_tops = score_cut(own, after, cut, next_tops)
            sums = mix_cut(pair, cut, tops, sums)
        for j in range(per_pair):
            h = pair * per_pair + j
            share = 1.0 / sums[j][head : head + SUB, :]
            mixed = sums[j][:head, :].reshape(head // SUB, SUB, TILE) * share[None]
            att_ref[h * head : (h + 1) * head, :] = mixed.reshape(head, TILE)
        return next_tops

    def join(t):
        attended = att_ref[...].T.astype(BF16)
        stream = x_ref[tile_at(t), :].astype(F32) + dot(attended, out_w[...])
        sum_ref[...] = stream
        mid_ref[...] = layer_norm(stream, gains[1:2, :]).astype(BF16)

    def mlp_piece(i):
        cut = slice(i * piece, (i + 1) * piece)
        inner = gelu(dot(mid_ref[...], up_w[:, cut])).astype(BF16)
        sum_ref[...] += dot(inner, down_w[cut, :])

    def attend_tile(t, tops, after, beside):
        for i in range(pairs):
            tops = attend_pair(i, tops, t if i + 1 < pairs else after)
            if beside:
                mlp_piece(i)
        return tops

    def step(t, tops):
        join(t - 1)
        tops = attend_tile(t, tops, jnp.minimum(t + 1, high - 1), True)
        y_ref[tile_at(t - 1), :] = sum_ref[...].astype(BF16)
        return tops

    own = masked_queries(low, 0)
    tops = None
    for cut in cuts:
        tops = score_cut(own, 0, cut, tops)
    tops = attend_tile(low, tops, low + 1 if high > low + 1 else None, False)
    if high > low + 1:
        lax.fori_loop(low + 1, high, step, tops)
    join(high - 1)
    for i in range(pairs):
        mlp_piece(i)
    y_ref[tile_at(high - 1), :] = sum_ref[...].astype(BF16)


def start_loads(block, hbm, vmem, sems):
    copies = [
        pltpu.make_async_copy(src.at[block], dst, sems.at[i])
        for i, (src, dst) in enumerate(zip(hbm, vmem))
    ]
    for copy in copies:
        copy.start()
    return copies


def pack_kernel(me_ref, hil_ref, z_ref, x_ref, out_ref, ids_ref, *, parts):
    rows, width = x_ref.shape
    n_dev = out_ref.shape[0]
    part_rows = rows // parts
    shift = log2(rows)
    z = z_ref[...]
    pair = jnp.concatenate([(z >> shift) + 1, (z & (rows - 1)) >> log2(GROUP)], axis=0)
    meta = jnp.concatenate([pair] * (SUB // 2), axis=0).astype(F32).astype(BF16)
    places, counts, starts = sort_places(hil_ref[...] >> shift, n_dev, rows, parts)
    slot_row = part_slots(counts, starts, part_rows, parts)
    ids_ref[...] = jnp.zeros_like(ids_ref)
    for q in range(parts):
        hot = one_hot(places - q * part_rows == iota((part_rows, rows), 0))
        sorted_rows = dot(hot, x_ref[...]).astype(BF16)
        ids = dot(meta, hot, NT)
        ids = jnp.where(iota(ids.shape, 0) // 2 == q, ids, 0.0).astype(BF16)
        emit_rows(slot_row, sorted_rows, ids, q, out_ref, ids_ref)
    emit_ids(me_ref[0], out_ref, ids_ref)


def emit_block(me, groups, base, slot_row, y_ref, parents, send_ref, ids_ref):
    part_rows = slot_row.shape[1]
    for g in groups:
        at = slice(g * part_rows, (g + 1) * part_rows)
        meta = parents[:, at]
        meta = jnp.where(iota(meta.shape, 0) == g - base, meta, 0.0).astype(BF16)
        emit_rows(slot_row, y_ref[at, :], meta, g - base, send_ref, ids_ref)
    emit_ids(me, send_ref, ids_ref)


def open_kernel(me_ref, got_ref, parent_ref, gains_ref, *refs, parts, split):
    hbm, refs = refs[:4], refs[4:]
    if split:
        (send_ref, x_out, qk_out, vt_out, ids_out, slot_out), refs = refs[:6], refs[6:]
    else:
        (send_ref,), refs = refs[:1], refs[1:]
    x_ref, y_ref, parents_ref, ids_ref = refs[:4]
    state, weights, sems, out_sems = refs[4:10], refs[10:14], refs[14], refs[15]
    qk_ref, vt_ref = state[:2]
    rows, width = x_ref.shape
    n_dev = got_ref.shape[0]
    part_rows = rows // parts
    lanes_of = width // LANES
    loads = start_loads(0, hbm, weights, sems)
    gains = gains_ref[0]
    fill_ones(vt_ref)

    ids = slot_ids(got_ref)
    dest = jnp.concatenate([ids[2 * g : 2 * g + 1, :] for g in range(parts)], axis=1).astype(I32) - 1
    parents = jnp.concatenate([ids[2 * g + 1 : 2 * g + 2, :] for g in range(parts)], axis=1) + 1.0
    parents = jnp.broadcast_to(parents, (SUB, parents.shape[1])).astype(BF16)
    places, counts, starts = sort_places(dest, n_dev, rows, parts)
    slot_row = part_slots(counts, starts, part_rows, parts)

    loads[0].wait()

    def receive(t, carry):
        hot = one_hot(places - t * TILE == iota((TILE, places.shape[1]), 0))
        for c in range(0, lanes_of, 2):
            data = jnp.concatenate([slot_rows_cut(got_ref, g, c, lanes_of) for g in range(parts)], axis=0)
            x_ref[tile_at(t), c * LANES : (c + 2) * LANES] = dot(hot, data).astype(BF16)
        parents_ref[:, tile_at(t)] = dot(parents, hot, NT)
        return carry

    lax.fori_loop(0, rows // TILE, receive, 0)

    def project(t, carry):
        project_tile(t, x_ref, qk_ref, vt_ref, weights[0], gains)
        return carry

    lax.fori_loop(0, rows // TILE, project, 0)
    saves = []
    if split:
        ids_out[...] = parents_ref[...]
        slot_out[...] = jnp.broadcast_to(slot_row, slot_out.shape)
        saves = [
            pltpu.make_async_copy(src, dst, out_sems.at[i])
            for i, (src, dst) in enumerate(((x_ref, x_out), (qk_ref, qk_out), (vt_ref, vt_out)))
        ]
        for save in saves:
            save.start()
    for load in loads[1:]:
        load.wait()
    groups = 1 if split else parts
    run_tiles(0, groups * part_rows // TILE, x_ref, y_ref, state, weights, gains)

    ids_ref[...] = jnp.zeros_like(ids_ref)
    parent = parent_ref[...]
    label_slot = group_slots(parent, n_dev, PART)
    low = (parent & (parent.shape[1] - 1)) + 1
    low = jnp.broadcast_to(low, (SUB, low.shape[1])).astype(F32)
    low = jnp.where(iota(low.shape, 0) == LABEL_ROW, low, 0.0).astype(BF16)
    for t in range(ids_ref.shape[1] // TILE):
        hot = one_hot(label_slot - t * TILE == iota((TILE, label_slot.shape[1]), 0))
        ids_ref[:, tile_at(t)] += dot(low, hot, NT)
    emit_block(me_ref[0], range(groups), 0, slot_row, y_ref, parents_ref[...], send_ref, ids_ref)
    for save in saves:
        save.wait()


def slot_rows_cut(got_ref, group, c, lanes_of):
    n_dev, depth, _ = got_ref.shape
    span = (depth - SUB) // lanes_of
    return jnp.concatenate(
        [
            got_ref[:, j * span + group * PART : j * span + (group + 1) * PART, :].reshape(n_dev * PART, LANES)
            for j in (c, c + 1)
        ],
        axis=1,
    )


def rest_kernel(me_ref, x_ref, qk_ref, vt_ref, parents_ref, slot_ref, gains_ref, *refs, parts):
    hbm, send_ref, y_ref, ids_ref = refs[:4], refs[4], refs[5], refs[6]
    scratch, weights, sems = refs[7:11], refs[11:14], refs[14]
    loads = start_loads(0, hbm[1:], weights, sems)
    for load in loads:
        load.wait()
    rows = x_ref.shape[0]
    run_tiles(
        rows // parts // TILE, rows // TILE, x_ref, y_ref, (qk_ref, vt_ref, *scratch), (None, *weights), gains_ref[0]
    )
    ids_ref[...] = jnp.zeros_like(ids_ref)
    emit_block(me_ref[0], range(1, parts), 1, slot_ref[0:1, :], y_ref, parents_ref[...], send_ref, ids_ref)


def second_kernel(*refs, parts, chunks, cap_groups):
    got_refs, refs = refs[:chunks], refs[chunks:]
    (parent_ref, gains_ref), hbm, (send_ref, label_ref), refs = refs[:2], refs[2:6], refs[6:8], refs[8:]
    x_ref, y_ref, parents_ref = refs[:3]
    state, weights, sems = refs[3:9], refs[9:13], refs[13]
    rows, width = x_ref.shape
    n_dev = got_refs[0].shape[0]
    part_rows = rows // parts
    loads = start_loads(1, hbm, weights, sems)
    gains = gains_ref[1]
    fill_ones(state[1])

    part = 0
    for k, got_ref in enumerate(got_refs):
        ids = slot_ids(got_ref)
        if k == 0:
            slots = n_dev * cap_groups
            wide, slim = iota((n_dev * PART, slots), 0), iota((n_dev * PART, slots), 1)
            order = slim & (cap_groups - 1)
            narrow = one_hot(wide == (slim >> log2(cap_groups)) * PART + order)
            label_ref[...] = dot(ids.astype(BF16), narrow)
        for g in range(parts if chunks == 1 else (1, parts - 1)[k]):
            own = ids[g : g + 1, :]
            ranks, _ = rank_rows(jnp.where(own > 0.0, 0, -1), SUB)
            places = jnp.concatenate([pick(hot, run) for hot, run in ranks], axis=1).astype(I32) - 1
            own = jnp.broadcast_to(own, ids.shape).astype(BF16)
            for t in range(part_rows // TILE):
                hot = one_hot(places - t * TILE == iota((TILE, places.shape[1]), 0))
                at = tile_at(part * (part_rows // TILE) + t)
                x_ref[at, :] = dot(hot, slot_rows(got_ref, g, width // LANES)).astype(BF16)
                parents_ref[:, at] = dot(own, hot, NT)
            part += 1

    loads[0].wait()

    def project(t, carry):
        project_tile(t, x_ref, state[0], state[1], weights[0], gains)
        return carry

    lax.fori_loop(0, rows // TILE, project, 0)
    for load in loads[1:]:
        load.wait()
    run_tiles(0, rows // TILE, x_ref, y_ref, state, weights, gains)

    groups = rows // GROUP
    member = one_hot(parents_ref[0:1, :].astype(I32) - 1 == iota((groups, rows), 0))
    sums = dot(member, y_ref[...]).astype(BF16)
    slot = group_slots(parent_ref[...], n_dev, cap_groups)
    send_ref[...] = dot(one_hot(slot == iota((send_ref.shape[0], groups), 0)), sums).astype(BF16)


def pool_kernel(label_ref, got_ref, out_ref):
    label = label_ref[LABEL_ROW : LABEL_ROW + 1, :].astype(I32) - 1
    hot = one_hot(label == iota((out_ref.shape[0], label.shape[1]), 0))
    out_ref[...] = dot(hot, got_ref[...])


VMEM = pl.BlockSpec(memory_space=pltpu.VMEM)
SMEM = pl.BlockSpec(memory_space=pltpu.SMEM)
ANY = pl.BlockSpec(memory_space=pl.ANY)


def call(body, name, outs, in_specs, out_specs=VMEM, scratch=(), flops=0):
    return pl.pallas_call(
        body,
        out_shape=outs,
        in_specs=in_specs,
        out_specs=out_specs,
        scratch_shapes=list(scratch),
        compiler_params=pltpu.CompilerParams(vmem_limit_bytes=56 * 1024 * 1024),
        cost_estimate=pl.CostEstimate(flops=flops, bytes_accessed=flops // 300, transcendentals=0),
        name=name,
    )


def exchange(data):
    return lax.all_to_all(data, "vox", split_axis=0, concat_axis=0, tiled=True)


def shards(
    voxels, hilbert_rank, z_rank, parent_slot, qkv_weight, out_weight, up_weight, down_weight, norm_gains
):
    rows, width = voxels.shape
    n_dev = lax.axis_size("vox")
    me = lax.axis_index("vox").astype(I32).reshape(1)
    cap = 2 * max(rows // n_dev, 1)
    parts = max(cap // PART, 1)
    groups = rows // GROUP
    cap_groups = 2 * max(groups // n_dev, 1)
    lanes_of = width // LANES
    weights = (qkv_weight, out_weight, up_weight, down_weight)
    weight_scratch = [pltpu.VMEM(w.shape[1:], BF16) for w in weights]
    parent = parent_slot.reshape(1, groups)
    full_flops = 9_000_000 * rows

    def slots(part_count):
        return jax.ShapeDtypeStruct((n_dev, lanes_of * part_count * PART + SUB, LANES), BF16)

    qk = ((rows, 2 * width), BF16)
    vt = ((HEADS, width // HEADS + ONES, rows), BF16)
    tile_scratch = [
        pltpu.VMEM((width, TILE), F32),
        pltpu.VMEM((TILE, width), BF16),
        pltpu.VMEM((TILE, width), F32),
        pltpu.VMEM((2, LANES * HEADS // width, rows, TILE), F32),
    ]
    patch = pltpu.VMEM((rows, width), BF16)
    id_rows = pltpu.VMEM((SUB, rows), F32)
    slot_ids_scratch = pltpu.VMEM((SUB, n_dev * PART), F32)

    send = call(
        functools.partial(pack_kernel, parts=parts),
        "pack",
        slots(parts),
        [SMEM, VMEM, VMEM, VMEM],
        scratch=[slot_ids_scratch],
    )(me, hilbert_rank.reshape(1, rows), z_rank.reshape(1, rows), voxels)
    got = exchange(send)

    split = parts > 1
    outs, specs = [slots(1 if split else parts)], [VMEM]
    if split:
        outs += [
            jax.ShapeDtypeStruct((rows, width), BF16),
            jax.ShapeDtypeStruct(*qk),
            jax.ShapeDtypeStruct(*vt),
            jax.ShapeDtypeStruct((SUB, rows), F32),
            jax.ShapeDtypeStruct((SUB, rows // parts), I32),
        ]
        specs += [ANY, ANY, ANY, VMEM, VMEM]
    sends = call(
        functools.partial(open_kernel, parts=parts, split=split),
        "open",
        outs,
        [SMEM, VMEM, VMEM, VMEM, ANY, ANY, ANY, ANY],
        specs,
        scratch=[
            patch,
            patch,
            id_rows,
            slot_ids_scratch,
            pltpu.VMEM(*qk),
            pltpu.VMEM(*vt),
            *tile_scratch,
            *weight_scratch,
            pltpu.SemaphoreType.DMA((4,)),
            pltpu.SemaphoreType.DMA((3,)),
        ],
        flops=full_flops // 2,
    )(me, got, parent, norm_gains, *weights)
    gots = [exchange(sends[0])]
    if split:
        send = call(
            functools.partial(rest_kernel, parts=parts),
            "rest",
            slots(parts - 1),
            [SMEM, VMEM, VMEM, VMEM, VMEM, VMEM, VMEM, ANY, ANY, ANY, ANY],
            scratch=[
                patch,
                slot_ids_scratch,
                *tile_scratch,
                *weight_scratch[1:],
                pltpu.SemaphoreType.DMA((3,)),
            ],
            flops=full_flops // 2,
        )(me, *sends[1:], norm_gains, *weights)
        gots.append(exchange(send))

    send, label = call(
        functools.partial(second_kernel, parts=parts, chunks=len(gots), cap_groups=cap_groups),
        "second",
        [
            jax.ShapeDtypeStruct((n_dev * cap_groups, width), BF16),
            jax.ShapeDtypeStruct((SUB, n_dev * cap_groups), F32),
        ],
        [VMEM] * (len(gots) + 2) + [ANY] * 4,
        [VMEM, VMEM],
        scratch=[
            patch,
            patch,
            id_rows,
            pltpu.VMEM(*qk),
            pltpu.VMEM(*vt),
            *tile_scratch,
            *weight_scratch,
            pltpu.SemaphoreType.DMA((4,)),
        ],
        flops=full_flops,
    )(*gots, parent, norm_gains, *weights)
    got = exchange(send.reshape(n_dev, cap_groups, width)).reshape(n_dev * cap_groups, width)
    return call(
        pool_kernel,
        "pool",
        jax.ShapeDtypeStruct((groups, width), F32),
        [VMEM, VMEM],
    )(label, got)


def solution(mesh):
    placed = (P("vox", None), P("vox"), P("vox"), P("vox"), P(), P(), P(), P(), P())
    return jax.shard_map(
        shards, mesh=mesh, in_specs=placed, out_specs=P("vox", None), check_vma=False
    )
```

profile of v0, /device:TPU:0, one launch (start us, length us, event | category | flops | bytes accessed | tf_op | source)
XLA Modules:
  0.0 190.2 jit_solution(18320347903056744948)
XLA Ops:
  0.0 6.0 %pack.1 = bf16[32,264,128]{2,1,0:T(8,128)(2,1)} custom-call(s32[1]{0:T(128)} %bitcast.me_ref, s32[1,1024]{1,0:T(1,128)} %bitcast.8, s32[1,1024]{1,0:T(1,128)} %bitcast.9, bf16[1024,512]{1,0:T(8,128)(2,1)} %x_ref.1), custom_call_target="tpu_custom_call" | custom-call | tf_op jit(solution)/shard_map/pack/pallas_call | solution.py:524
  6.0 59.2 %all_to_all.20.got_ref = bf16[32,264,128]{2,1,0:T(8,128)(2,1)} all-to-all(bf16[32,264,128]{2,1,0:T(8,128)(2,1)} %pack.1), channel_id=1, replica_groups=mesh['vox'=32] {'vox'}, dimensions={0} | all-to-all | bytes 4325376 | tf_op jit(solution)/shard_map/all_to_all | solution.py:490
  65.2 16.8 %open.1 = (bf16[32,72,128]{2,1,0:T(8,128)(2,1)}, bf16[1024,512]{1,0:T(8,128)(2,1)}, bf16[1024,1024]{1,0:T(8,128)(2,1)}, bf16[8,80,1024]{2,1,0:T(8,128)(2,1)}, f32[8,1024]{1,0:T(8,128)}, /*index=5*/s32[8,256]{1,0:T(8,128)}) custom-call(s32[1]{0:T(128)} %bitcast.me_ref, bf16[32,264,128]{2,1,0:T(8,128)(2,1)} %all_to_all.20.got_ref, s32[1,128]{1,0:T(1,128)} %bitcast.10, ...), custom_call_target="tpu_custom_call" | custom-call | flops 4608000000 | bytes 15360000 | tf_op jit(solution)/shard_map/open/pallas_call | solution.py:544
  82.0 2.8 %all-to-all-start.1 = ((bf16[32,72,128]{2,1,0:T(8,128)(2,1)}), bf16[32,72,128]{2,1,0:T(8,128)(2,1)S(1)}, u32[]{:S(2)}, u32[]{:S(2)}) async-start(bf16[32,72,128]{2,1,0:T(8,128)(2,1)} %get-tuple-element.13), calls=%async_computation.1 | async-start | bytes 1179648 | tf_op jit(solution)/shard_map/all_to_all | solution.py:490
  84.8 19.7 %rest.1 = bf16[32,200,128]{2,1,0:T(8,128)(2,1)} custom-call(s32[1]{0:T(128)} %bitcast.me_ref, bf16[1024,512]{1,0:T(8,128)(2,1)} %get-tuple-element.14.x_ref, bf16[1024,1024]{1,0:T(8,128)(2,1)} %get-tuple-element.15.qk_ref, bf16[8,80,1024]{2,1,0:T(8,128)(2,1)} %get-tuple-element.16.vt_ref, f32[8,1024]{1,0:T(8,128)} %get-tuple-element.17.parents_ref, ...), custom_call_target="tpu_custom_call" | custom-call | flops 4608000000 | bytes 15360000 | tf_op jit(solution)/shard_map/rest/pallas_call | solution.py:566
  104.5 0.0 all-to-all-done.1.refs_0_
  104.6 0.0 copy-start
  104.6 45.0 %all_to_all.21.refs_1_ = bf16[32,200,128]{2,1,0:T(8,128)(2,1)} all-to-all(bf16[32,200,128]{2,1,0:T(8,128)(2,1)} %rest.1), channel_id=1, replica_groups=mesh['vox'=32] {'vox'}, dimensions={0} | all-to-all | bytes 3276800 | tf_op jit(solution)/shard_map/all_to_all | solution.py:490
  149.6 0.0 copy-done
  149.6 24.8 %second.1 = (bf16[256,512]{1,0:T(8,128)(2,1)}, f32[8,256]{1,0:T(8,128)}) custom-call(bf16[32,72,128]{2,1,0:T(8,128)(2,1)} %copy-done, bf16[32,200,128]{2,1,0:T(8,128)(2,1)} %all_to_all.21.refs_1_, s32[1,128]{1,0:T(1,128)} %bitcast.11, f32[2,2,512]{2,1,0:T(2,128)} %refs_3_.5, bf16[2,512,1536]{2,1,0:T(8,128)(2,1)} %refs_4_.1, bf16[2,512,512]{2,1,0:T(8,128)(2,1)} %refs_5_.1, ...), custom_call_target="tpu_custom_call" | custom-call | flops 9216000000 | bytes 30720000 | tf_op jit(solution)/shard_map/second/pallas_call | solution.py:582
  174.4 13.9 %all_to_all.22 = bf16[32,8,512]{2,1,0:T(8,128)(2,1)} all-to-all(bf16[32,8,512]{2,1,0:T(8,128)(2,1)} %bitcast.7), channel_id=1, replica_groups=mesh['vox'=32] {'vox'}, dimensions={0} | all-to-all | bytes 524288 | tf_op jit(solution)/shard_map/all_to_all | solution.py:490
  188.3 1.9 pool.1
Async XLA Ops:
  82.0 22.5 %all-to-all-start.1 = ((bf16[32,72,128]{2,1,0:T(8,128)(2,1)}), bf16[32,72,128]{2,1,0:T(8,128)(2,1)S(1)}, u32[]{:S(2)}, u32[]{:S(2)}) async-start(bf16[32,72,128]{2,1,0:T(8,128)(2,1)} %get-tuple-element.13), calls=%async_computation.1 | async-start | bytes 1179648 | tf_op jit(solution)/shard_map/all_to_all | solution.py:490
  104.6 45.1 %copy-start = (bf16[32,72,128]{2,1,0:T(8,128)(2,1)}, bf16[32,72,128]{2,1,0:T(8,128)(2,1)S(1)}, u32[]{:S(2)}) copy-start(bf16[32,72,128]{2,1,0:T(8,128)(2,1)S(1)} %all-to-all-done.1.refs_0_) | copy-start | bytes 1769476
where the time goes:
time: 191 us; the launch traced here: 190 us
  blocking collectives  118 us (62%)
  Pallas kernels  69.1 us (36%)
  starting transfers between devices  2.81 us (1%)
    all_to_all x3, blocking collectives, exchange(): return lax.all_to_all(data, 'vox', split_axis=0, concat_axis=0, tiled=True)  118 us
    pallas_call x1, Pallas kernels, shards(): call(functools.partial(second_kernel, parts=parts, chunks=len(gots), cap_...  24.8 us
    pallas_call x1, Pallas kernels, shards(): call(functools.partial(rest_kernel, parts=parts), 'rest', slots(parts - 1...  19.7 us
    pallas_call x1, Pallas kernels, shards(): call(functools.partial(open_kernel, parts=parts, split=split), 'open', ou...  16.8 us
    pallas_call x1, Pallas kernels, shards(): call(functools.partial(pack_kernel, parts=parts), 'pack', slots(parts), [...  5.95 us
  transfers between devices with their start and end apart: 1, of which 0 were waited for; matrix products, arithmetic and copies ran while one was open for 0% of the time, Pallas kernels for 10%

commit v1 on v0

v1 whole, which is shorter than its diff:
```python
import functools

import jax
import jax.numpy as jnp
from jax import lax
from jax.experimental import pallas as pl
from jax.experimental.pallas import tpu as pltpu
from jax.sharding import PartitionSpec as P

HEADS = 8
LANES = 128
SUB = 8
GROUP = 8
TILE = 256
PART = 16
LABEL_ROW = 7
F32 = jnp.float32
BF16 = jnp.bfloat16
I32 = jnp.int32
LOG2E = 1.4426950408889634
GELU_C = 0.7978845608028654
ONES = 16
NT = (((1,), (1,)), ((), ()))


def dot(a, b, dims=(((1,), (0,)), ((), ()))):
    return lax.dot_general(a, b, dims, preferred_element_type=F32)


def iota(shape, axis):
    return lax.broadcasted_iota(I32, shape, axis)


def one_hot(mask):
    return mask.astype(F32).astype(BF16)


def log2(value):
    bits = value.bit_length() - 1
    assert 1 << bits == value
    return bits


def tile_at(t):
    return pl.ds(t * TILE if isinstance(t, int) else pl.multiple_of(t * TILE, TILE), TILE)


def lane_cuts(size):
    return range(0, size, LANES)


def rank_rows(dest, n_dev):
    tri = (iota((LANES, LANES), 0) <= iota((LANES, LANES), 1)).astype(F32)
    tri = jnp.concatenate([tri, jnp.ones((LANES, LANES), F32)], axis=1).astype(BF16)
    dev = iota((n_dev, LANES), 0)
    seen = jnp.zeros((n_dev, LANES), F32)
    chunks = []
    for at in lane_cuts(dest.shape[1]):
        hot = (dest[:, at : at + LANES] == dev).astype(F32)
        both = dot(hot.astype(BF16), tri)
        chunks.append((hot, both[:, :LANES] + seen))
        seen = seen + both[:, LANES:]
    return chunks, seen


def pick(hot, table):
    return jnp.sum(hot * table, axis=0, keepdims=True)


def part_starts(counts, parts):
    n_dev = counts.shape[0]
    below = one_hot(iota((n_dev, n_dev), 1) < iota((n_dev, n_dev), 0))
    return dot(below, counts.astype(BF16)) * (1.0 / parts)


def sort_places(dest, n_dev, rows, parts):
    chunks, counts = rank_rows(dest, n_dev)
    starts = part_starts(counts, parts)
    part_rows = rows // parts
    cap = parts * PART
    places = []
    for hot, run in chunks:
        order = pick(hot, run - 1).astype(I32)
        count = pick(hot, counts).astype(I32)
        start = pick(hot, starts).astype(I32)
        full = count == cap
        part = jnp.where(full, order >> log2(PART), order >> log2(PART // 2))
        inside = order - part * jnp.where(full, PART, PART // 2)
        places.append(jnp.where(count > 0, part * part_rows + start + inside, -1))
    return jnp.concatenate(places, axis=1), counts, starts


def part_slots(counts, starts, part_rows, parts):
    n_dev = counts.shape[0]
    share = counts * (1.0 / parts)
    dev = iota((n_dev, LANES), 0).astype(F32) * PART
    slots = []
    for at in lane_cuts(part_rows):
        k = (iota((n_dev, LANES), 1) + at).astype(F32)
        inside = ((k >= starts) & (k < starts + share)).astype(F32)
        slots.append(pick(inside, dev + k - starts))
    return jnp.concatenate(slots, axis=1).astype(I32)


def group_slots(parent, n_dev, stride):
    chunks, _ = rank_rows(parent >> log2(parent.shape[1]), n_dev)
    dev = iota((n_dev, LANES), 0).astype(F32) * stride
    return jnp.concatenate([pick(hot, run - 1 + dev) for hot, run in chunks], axis=1).astype(I32)


def emit_rows(slot_row, rows, group, out_ref):
    lanes_of = rows.shape[1] // LANES
    for t in range(out_ref.shape[0] * PART // TILE):
        hot = one_hot(slot_row - t * TILE == iota((TILE, slot_row.shape[1]), 0))
        placed = dot(hot, rows).astype(BF16)
        for d in range(TILE // PART):
            for c in range(lanes_of):
                at = (group * lanes_of + c) * PART
                out_ref[t * (TILE // PART) + d, at : at + PART, :] = placed[
                    d * PART : (d + 1) * PART, c * LANES : (c + 1) * LANES
                ]


def place_ids(slot_row, meta, ids_ref):
    for t in range(ids_ref.shape[1] // TILE):
        hot = one_hot(slot_row - t * TILE == iota((TILE, slot_row.shape[1]), 0))
        ids_ref[:, tile_at(t)] += dot(meta, hot, NT)


def emit_ids(me, out_ref, ids_ref):
    per_tile = LANES // PART
    mine = lax.rem(me, per_tile)
    owned = iota((SUB, LANES), 1) // PART == mine
    at = out_ref.shape[1] - SUB
    for dev in range(out_ref.shape[0]):
        cut = dev // per_tile * LANES
        turn = lax.rem(mine + (per_tile - dev % per_tile), per_tile) * PART
        part = pltpu.roll(ids_ref[:, cut : cut + LANES], turn, 1)
        out_ref[dev, at:, :] = jnp.where(owned, part, 0.0).astype(BF16)


def slot_ids(got_ref):
    n_dev, depth, _ = got_ref.shape
    per_tile = LANES // PART
    tiles = []
    for first in range(0, n_dev, per_tile):
        total = got_ref[first, depth - SUB :, :].astype(F32)
        for j in range(1, per_tile):
            total = total + got_ref[first + j, depth - SUB :, :].astype(F32)
        tiles.append(total)
    return jnp.concatenate(tiles, axis=1)


def slot_rows(got_ref, group, lanes_of, first=0, count=None):
    n_dev = got_ref.shape[0]
    count = lanes_of if count is None else count
    return jnp.concatenate(
        [
            got_ref[:, (group * lanes_of + c) * PART : (group * lanes_of + c + 1) * PART, :].reshape(
                n_dev * PART, LANES
            )
            for c in range(first, first + count)
        ],
        axis=1,
    )


def start_all(pairs, sems, first=0):
    copies = [pltpu.make_async_copy(src, dst, sems.at[first + i]) for i, (src, dst) in enumerate(pairs)]
    for copy in copies:
        copy.start()
    return copies


def wait_all(copies):
    for copy in copies:
        copy.wait()


def slot_loads(got_hbm, got_ref, sems, first=0):
    at = got_ref.shape[1] - SUB
    return start_all(
        [(got_hbm.at[:, at:, :], got_ref.at[:, at:, :]), (got_hbm.at[:, :at, :], got_ref.at[:, :at, :])], sems, first
    )


def layer_norm(stream, gain_row):
    row_mean = jnp.mean(stream, axis=-1, keepdims=True)
    centred = stream - row_mean
    row_var = jnp.mean(centred * centred, axis=-1, keepdims=True)
    return centred * lax.rsqrt(row_var + 1e-05) * gain_row


def gelu(x):
    inner = x * (x * x * (0.044715 * GELU_C) + GELU_C)
    half = 0.5 * x
    return half + half * jnp.tanh(inner)


def project_tile(t, x_ref, qk_ref, vt_ref, qkv_w, gains):
    width = x_ref.shape[1]
    head = width // HEADS
    at = tile_at(t)
    normed = layer_norm(x_ref[at, :].astype(F32), gains[0:1, :]).astype(BF16)
    qk_ref[at, :width] = (dot(normed, qkv_w[:, :width]) * (LOG2E * head**-0.5)).astype(BF16)
    qk_ref[at, width:] = dot(normed, qkv_w[:, width : 2 * width]).astype(BF16)
    values = dot(normed, qkv_w[:, 2 * width :]).T.astype(BF16)
    for h in range(HEADS):
        vt_ref[h, :head, at] = values[h * head : (h + 1) * head, :]


def fill_ones(vt_ref):
    depth = vt_ref.shape[1]
    for h in range(HEADS):
        vt_ref[h, depth - ONES :, :] = jnp.ones((ONES, vt_ref.shape[2]), BF16)


def run_tiles(low, high, x_ref, y_ref, state, weights, gains, before_mix=(), before_join=()):
    qk_ref, vt_ref, att_ref, mid_ref, sum_ref, score_ref = state
    _, out_w, up_w, down_w = weights
    rows, width = x_ref.shape
    head = width // HEADS
    pairs = width // LANES
    per_pair = LANES // head
    piece = up_w.shape[1] // pairs
    owner = iota((TILE, LANES), 1) // head
    cuts = [slice(at, at + TILE) for at in range(0, rows, TILE)]

    def masked_queries(t, pair):
        queries = qk_ref[tile_at(t), pair * LANES : (pair + 1) * LANES]
        return [jnp.where(owner == j, queries, jnp.zeros_like(queries)) for j in range(per_pair)]

    def score(own, pair, cut):
        key_rows = qk_ref[cut, width + pair * LANES : width + (pair + 1) * LANES]
        return [dot(key_rows, own[j], NT) for j in range(per_pair)]

    def keep(scores, pair, cut, tops):
        result = []
        for j in range(per_pair):
            score_ref[pair % 2, j, cut, :] = scores[j]
            top = jnp.max(scores[j].reshape(TILE // SUB, SUB, TILE), axis=0)
            result.append(top if tops is None else jnp.maximum(tops[j], top))
        return result

    def soften(pair, cut, tops):
        return [jnp.exp2(score_ref[pair % 2, j, cut, :] - tops[j]).astype(BF16) for j in range(per_pair)]

    def mix(pair, cut, probs, sums):
        result = []
        for j in range(per_pair):
            mixed = dot(vt_ref[pair * per_pair + j, :, cut], probs[j])
            result.append(mixed if sums is None else sums[j] + mixed)
        return result

    def attend_pair(pair, tops, next_tile):
        after = (pair + 1) % pairs
        own = None if next_tile is None else masked_queries(next_tile, after)
        tops = [jnp.max(top, axis=0, keepdims=True) for top in tops]
        next_tops, sums = None, None
        for cut in cuts:
            scores = None if own is None else score(own, after, cut)
            probs = soften(pair, cut, tops)
            if own is not None:
                next_tops = keep(scores, after, cut, next_tops)
            sums = mix(pair, cut, probs, sums)
        for j in range(per_pair):
            h = pair * per_pair + j
            share = 1.0 / sums[j][head : head + SUB, :]
            mixed = sums[j][:head, :].reshape(head // SUB, SUB, TILE) * share[None]
            att_ref[h * head : (h + 1) * head, :] = mixed.reshape(head, TILE)
        return next_tops

    def join(t):
        attended = att_ref[...].T.astype(BF16)
        stream = x_ref[tile_at(t), :].astype(F32) + dot(attended, out_w[...])
        sum_ref[...] = stream
        mid_ref[...] = layer_norm(stream, gains[1:2, :]).astype(BF16)

    def mlp_piece(i):
        cut = slice(i * piece, (i + 1) * piece)
        inner = gelu(dot(mid_ref[...], up_w[:, cut])).astype(BF16)
        sum_ref[...] += dot(inner, down_w[cut, :])

    def attend_tile(t, tops, after, beside):
        for i in range(pairs):
            tops = attend_pair(i, tops, t if i + 1 < pairs else after)
            if beside:
                mlp_piece(i)
        return tops

    def step(t, tops):
        join(t - 1)
        tops = attend_tile(t, tops, jnp.minimum(t + 1, high - 1), True)
        y_ref[tile_at(t - 1), :] = sum_ref[...].astype(BF16)
        return tops

    own = masked_queries(low, 0)
    tops = None
    for cut in cuts:
        tops = keep(score(own, 0, cut), 0, cut, tops)
    wait_all(before_mix)
    tops = attend_tile(low, tops, low + 1 if high > low + 1 else None, False)
    wait_all(before_join)
    if high > low + 1:
        lax.fori_loop(low + 1, high, step, tops)
    join(high - 1)
    for i in range(pairs):
        mlp_piece(i)
    y_ref[tile_at(high - 1), :] = sum_ref[...].astype(BF16)


def pack_kernel(me_ref, hil_ref, z_ref, x_hbm, out_hbm, x_ref, out_ref, ids_ref, sems, *, parts):
    rows, width = x_ref.shape
    n_dev = out_ref.shape[0]
    span = width // LANES * PART
    loads = start_all([(x_hbm, x_ref)], sems)
    saves = []
    part_rows = rows // parts
    shift = log2(rows)
    z = z_ref[...]
    pair = jnp.concatenate([(z >> shift) + 1, (z & (rows - 1)) >> log2(GROUP)], axis=0)
    meta = jnp.concatenate([pair] * (SUB // 2), axis=0).astype(F32).astype(BF16)
    places, counts, starts = sort_places(hil_ref[...] >> shift, n_dev, rows, parts)
    slot_row = part_slots(counts, starts, part_rows, parts)
    wait_all(loads)
    total = None
    for q in range(parts):
        hot = one_hot(places - q * part_rows == iota((part_rows, rows), 0))
        sorted_rows = dot(hot, x_ref[...]).astype(BF16)
        ids = dot(meta, hot, NT)
        ids = jnp.where(iota(ids.shape, 0) // 2 == q, ids, 0.0)
        total = ids if total is None else total + ids
        emit_rows(slot_row, sorted_rows, q, out_ref)
        cut = pl.ds(q * span, span)
        saves += start_all([(out_ref.at[:, cut, :], out_hbm.at[:, cut, :])], sems, 1 + q)
    ids_ref[...] = jnp.zeros_like(ids_ref)
    place_ids(slot_row, total.astype(BF16), ids_ref)
    emit_ids(me_ref[0], out_ref, ids_ref)
    cut = pl.ds(parts * span, SUB)
    saves += start_all([(out_ref.at[:, cut, :], out_hbm.at[:, cut, :])], sems, 1 + parts)
    wait_all(saves)


def label_kernel(parent_ref, ids_ref, *, n_dev):
    parent = parent_ref[...]
    low = (parent & (parent.shape[1] - 1)) + 1
    low = jnp.broadcast_to(low, (SUB, low.shape[1])).astype(F32)
    low = jnp.where(iota(low.shape, 0) == LABEL_ROW, low, 0.0).astype(BF16)
    ids_ref[...] = jnp.zeros_like(ids_ref)
    place_ids(group_slots(parent, n_dev, PART), low, ids_ref)


def open_kernel(me_ref, got_hbm, label_ref, gains_ref, *refs, parts, split):
    hbm, refs = refs[:4], refs[4:]
    if split:
        (send_ref, x_out, qk_out, vt_out, slot_out), refs = refs[:5], refs[5:]
    else:
        (send_ref,), refs = refs[:1], refs[1:]
    x_ref, y_ref, parents_ref, ids_ref = refs[:4]
    state, weights, got_ref, sems, out_sems = refs[4:10], refs[10:14], refs[14], refs[15], refs[16]
    qk_ref, vt_ref = state[:2]
    rows, width = x_ref.shape
    n_dev = got_ref.shape[0]
    part_rows = rows // parts
    lanes_of = width // LANES
    gots = slot_loads(got_hbm, got_ref, sems)
    gains = gains_ref[0]
    fill_ones(vt_ref)

    gots[0].wait()
    ids = slot_ids(got_ref)
    dest = jnp.concatenate([ids[2 * g : 2 * g + 1, :] for g in range(parts)], axis=1).astype(I32) - 1
    parents = jnp.concatenate([ids[2 * g + 1 : 2 * g + 2, :] for g in range(parts)], axis=1) + 1.0
    parents = jnp.broadcast_to(parents, (SUB, parents.shape[1])).astype(BF16)
    places, counts, starts = sort_places(dest, n_dev, rows, parts)
    slot_row = part_slots(counts, starts, part_rows, parts)

    gots[1].wait()
    loads = start_all([(src.at[0], dst) for src, dst in zip(hbm, weights)], sems, 2)

    def receive(t, carry):
        hot = one_hot(places - t * TILE == iota((TILE, places.shape[1]), 0))
        for c in range(0, lanes_of, 2):
            data = jnp.concatenate([slot_rows(got_ref, g, lanes_of, c, 2) for g in range(parts)], axis=0)
            x_ref[tile_at(t), c * LANES : (c + 2) * LANES] = dot(hot, data).astype(BF16)
        parents_ref[:, tile_at(t)] = dot(parents, hot, NT)
        return carry

    lax.fori_loop(0, rows // TILE, receive, 0)
    loads[0].wait()

    def project(t, carry):
        project_tile(t, x_ref, qk_ref, vt_ref, weights[0], gains)
        return carry

    lax.fori_loop(0, rows // TILE, project, 0)
    saves = []
    if split:
        slot_out[...] = jnp.broadcast_to(slot_row, slot_out.shape)
        saves = start_all([(x_ref, x_out), (qk_ref, qk_out), (vt_ref, vt_out)], out_sems)
    groups = 1 if split else parts
    run_tiles(0, groups * part_rows // TILE, x_ref, y_ref, state, weights, gains, (), loads[1:])

    ids_ref[...] = label_ref[...]
    meta = [parents_ref[0:1, g * part_rows : (g + 1) * part_rows] for g in range(parts)]
    meta.append(jnp.zeros((SUB - parts, part_rows), F32))
    place_ids(slot_row, jnp.concatenate(meta, axis=0).astype(BF16), ids_ref)
    for g in range(groups):
        emit_rows(slot_row, y_ref[g * part_rows : (g + 1) * part_rows, :], g, send_ref)
    emit_ids(me_ref[0], send_ref, ids_ref)
    wait_all(saves)


def rest_kernel(x_hbm, qk_hbm, vt_hbm, slot_ref, gains_ref, *refs, parts):
    hbm, send_ref, (x_ref, y_ref, qk_ref, vt_ref), refs = refs[:4], refs[4], refs[5:9], refs[9:]
    scratch, weights, sems = refs[:4], refs[4:7], refs[7]
    low = x_ref.shape[0] // parts // TILE
    state = start_all(
        [
            (qk_hbm.at[tile_at(low), :], qk_ref.at[tile_at(low), :]),
            (qk_hbm.at[: low * TILE, :], qk_ref.at[: low * TILE, :]),
            (qk_hbm.at[(low + 1) * TILE :, :], qk_ref.at[(low + 1) * TILE :, :]),
            (vt_hbm, vt_ref),
            (x_hbm, x_ref),
        ],
        sems,
    )
    loads = start_all([(src.at[0], dst) for src, dst in zip(hbm[1:], weights)], sems, len(state))
    wait_all(state[:3])
    rows = x_ref.shape[0]
    run_tiles(
        low,
        rows // TILE,
        x_ref,
        y_ref,
        (qk_ref, vt_ref, *scratch),
        (None, *weights),
        gains_ref[0],
        state[3:4],
        state[4:] + loads,
    )
    part_rows = rows // parts
    for g in range(1, parts):
        emit_rows(slot_ref[0:1, :], y_ref[g * part_rows : (g + 1) * part_rows, :], g - 1, send_ref)


def receive_part(got_ref, group, places, own, at, x_ref, parents_ref):
    own = jnp.broadcast_to(own, (SUB, own.shape[1])).astype(BF16)
    lanes_of = x_ref.shape[1] // LANES
    for t in range(at.start // TILE, at.stop // TILE):
        hot = one_hot(places + (at.start - t * TILE) == iota((TILE, places.shape[1]), 0))
        x_ref[tile_at(t), :] = dot(hot, slot_rows(got_ref, group, lanes_of)).astype(BF16)
        parents_ref[:, tile_at(t)] = dot(own, hot, NT)


def index_kernel(got_hbm, parent_ref, gains_ref, qkv_hbm, *refs, parts, split, cap_groups):
    (places_ref, own_ref, label_ref, slot_ref), refs = refs[:4], refs[4:]
    if split:
        (x_out, qk_out, vt_out, parents_out), refs = refs[:4], refs[4:]
    got_ref, qkv_w, sems = refs[:3]
    gots = slot_loads(got_hbm, got_ref, sems)
    load = start_all([(qkv_hbm.at[1], qkv_w)], sems, 2)
    n_dev = got_ref.shape[0]
    span = n_dev * PART
    gots[0].wait()
    ids = slot_ids(got_ref)
    slots = n_dev * cap_groups
    wide, slim = iota((span, slots), 0), iota((span, slots), 1)
    narrow = one_hot(wide == (slim >> log2(cap_groups)) * PART + (slim & (cap_groups - 1)))
    label_ref[...] = dot(ids.astype(BF16), narrow)
    slot_ref[...] = jnp.broadcast_to(group_slots(parent_ref[...], n_dev, cap_groups), slot_ref.shape)
    for g in range(parts):
        own = ids[g : g + 1, :]
        ranks, _ = rank_rows(jnp.where(own > 0.0, 0, -1), SUB)
        places = jnp.concatenate([pick(hot, run) for hot, run in ranks], axis=1).astype(I32) - 1
        places_ref[g : g + 1, :] = places
        own_ref[g : g + 1, :] = own
    gots[1].wait()
    wait_all(load)
    if split:
        receive_part(got_ref, 0, places_ref[0:1, :], own_ref[0:1, :], slice(0, x_out.shape[0]), x_out, parents_out)
        for t in range(x_out.shape[0] // TILE):
            project_tile(t, x_out, qk_out, vt_out, qkv_w, gains_ref[1])


def second_kernel(*refs, parts, split):
    got_hbm, places_ref, own_ref, slot_ref, gains_ref, refs = refs[0], refs[1], refs[2], refs[3], refs[4], refs[5:]
    if split:
        early_hbm, refs = refs[:4], refs[4:]
    hbm, send_ref, refs = refs[:4], refs[4], refs[5:]
    x_ref, y_ref, parents_ref = refs[:3]
    state, weights, got_ref, sems = refs[3:9], refs[9:13], refs[13], refs[14]
    rows, width = x_ref.shape
    n_dev = got_ref.shape[0]
    part_rows = rows // parts
    first = 1 if split else 0
    gots = start_all([(got_hbm, got_ref), (hbm[0].at[1], weights[0])], sems)
    early = []
    gains = gains_ref[1]
    fill_ones(state[1])
    gots[0].wait()
    if split:
        values = width // HEADS
        early = start_all(
            [
                (early_hbm[0], x_ref.at[:part_rows, :]),
                (early_hbm[1], state[0].at[:part_rows, :]),
                (early_hbm[2], state[1].at[:, :values, :part_rows]),
                (early_hbm[3], parents_ref.at[:, :part_rows]),
            ],
            sems,
            5,
        )
    for g in range(first, parts):
        at = slice(g * part_rows, (g + 1) * part_rows)
        receive_part(got_ref, g - first, places_ref[g : g + 1, :], own_ref[g : g + 1, :], at, x_ref, parents_ref)
    gots[1].wait()
    loads = start_all([(src.at[1], dst) for src, dst in zip(hbm[1:], weights[1:])], sems, 2)

    def project(t, carry):
        project_tile(t, x_ref, state[0], state[1], weights[0], gains)
        return carry

    lax.fori_loop(first * part_rows // TILE, rows // TILE, project, 0)
    wait_all(early)
    run_tiles(0, rows // TILE, x_ref, y_ref, state, weights, gains, (), loads)

    groups = rows // GROUP
    member = one_hot(parents_ref[0:1, :].astype(I32) - 1 == iota((groups, rows), 0))
    sums = dot(member, y_ref[...]).astype(BF16)
    slot = slot_ref[0:1, :]
    send_ref[...] = dot(one_hot(slot == iota((send_ref.shape[0], groups), 0)), sums).astype(BF16)


def pool_kernel(label_ref, got_ref, out_ref):
    label = label_ref[LABEL_ROW : LABEL_ROW + 1, :].astype(I32) - 1
    hot = one_hot(label == iota((out_ref.shape[0], label.shape[1]), 0))
    out_ref[...] = dot(hot, got_ref[...])


VMEM = pl.BlockSpec(memory_space=pltpu.VMEM)
SMEM = pl.BlockSpec(memory_space=pltpu.SMEM)
ANY = pl.BlockSpec(memory_space=pltpu.HBM)


def call(body, name, outs, in_specs, out_specs=VMEM, scratch=(), flops=0):
    return pl.pallas_call(
        body,
        out_shape=outs,
        in_specs=in_specs,
        out_specs=out_specs,
        scratch_shapes=list(scratch),
        compiler_params=pltpu.CompilerParams(vmem_limit_bytes=66_000_000),
        cost_estimate=pl.CostEstimate(flops=flops, bytes_accessed=flops // 300, transcendentals=0),
        name=name,
    )


def exchange(data):
    return lax.all_to_all(data, "vox", split_axis=0, concat_axis=0, tiled=True)


def shards(
    voxels, hilbert_rank, z_rank, parent_slot, qkv_weight, out_weight, up_weight, down_weight, norm_gains
):
    rows, width = voxels.shape
    n_dev = lax.axis_size("vox")
    me = lax.axis_index("vox").astype(I32).reshape(1)
    cap = 2 * max(rows // n_dev, 1)
    parts = max(cap // PART, 1)
    groups = rows // GROUP
    cap_groups = 2 * max(groups // n_dev, 1)
    lanes_of = width // LANES
    weights = (qkv_weight, out_weight, up_weight, down_weight)
    weight_scratch = [pltpu.VMEM(w.shape[1:], BF16) for w in weights]
    parent = parent_slot.reshape(1, groups)
    full_flops = 9_000_000 * rows

    split = parts > 1

    def slots(part_count, with_ids=True):
        depth = lanes_of * part_count * PART + (SUB if with_ids else 0)
        return jax.ShapeDtypeStruct((n_dev, depth, LANES), BF16)

    def made(*shape, dtype=BF16):
        return jax.ShapeDtypeStruct(shape, dtype)

    head = width // HEADS
    part_rows = rows // parts
    qk = pltpu.VMEM((rows, 2 * width), BF16)
    vt = pltpu.VMEM((HEADS, head + ONES, rows), BF16)
    tile_scratch = [
        pltpu.VMEM((width, TILE), F32),
        pltpu.VMEM((TILE, width), BF16),
        pltpu.VMEM((TILE, width), F32),
        pltpu.VMEM((2, LANES // head, rows, TILE), F32),
    ]
    patch = pltpu.VMEM((rows, width), BF16)
    id_rows = pltpu.VMEM((SUB, rows), F32)
    slot_lanes = pltpu.VMEM((SUB, n_dev * PART), F32)
    first_slots, rest_slots = slots(1 if split else parts), slots(parts - 1, False)

    send = call(
        functools.partial(pack_kernel, parts=parts),
        "pack",
        slots(parts),
        [SMEM, VMEM, VMEM, ANY],
        ANY,
        scratch=[
            patch,
            pltpu.VMEM(slots(parts).shape, BF16),
            slot_lanes,
            pltpu.SemaphoreType.DMA((parts + 2,)),
        ],
    )(me, hilbert_rank.reshape(1, rows), z_rank.reshape(1, rows), voxels)
    got = exchange(send)
    labels = call(
        functools.partial(label_kernel, n_dev=n_dev),
        "label",
        made(SUB, n_dev * PART, dtype=F32),
        [VMEM],
        flops=full_flops // 16,
    )(parent)

    outs, specs = [first_slots], [VMEM]
    if split:
        outs += [made(rows, width), made(rows, 2 * width), made(HEADS, head + ONES, rows)]
        outs += [made(SUB, part_rows, dtype=I32)]
        specs += [ANY, ANY, ANY, VMEM]
    sends = call(
        functools.partial(open_kernel, parts=parts, split=split),
        "open",
        outs,
        [SMEM, ANY, VMEM, VMEM, ANY, ANY, ANY, ANY],
        specs,
        scratch=[
            patch,
            patch,
            id_rows,
            slot_lanes,
            qk,
            vt,
            *tile_scratch,
            *weight_scratch,
            pltpu.VMEM(slots(parts).shape, BF16),
            pltpu.SemaphoreType.DMA((6,)),
            pltpu.SemaphoreType.DMA((3,)),
        ],
        flops=full_flops // 2,
    )(me, got, labels, norm_gains, *weights)
    got = exchange(sends[0])
    if split:
        send = call(
            functools.partial(rest_kernel, parts=parts),
            "rest",
            rest_slots,
            [ANY, ANY, ANY, VMEM, VMEM, ANY, ANY, ANY, ANY],
            scratch=[
                patch,
                patch,
                qk,
                vt,
                *tile_scratch,
                *weight_scratch[1:],
                pltpu.SemaphoreType.DMA((8,)),
            ],
            flops=full_flops // 2,
        )(*sends[1:], norm_gains, *weights)
        late = exchange(send)

    outs = [
        made(SUB, n_dev * PART, dtype=I32),
        made(SUB, n_dev * PART, dtype=F32),
        made(SUB, n_dev * cap_groups, dtype=F32),
        made(SUB, groups, dtype=I32),
    ]
    if split:
        outs += [made(part_rows, width), made(part_rows, 2 * width), made(HEADS, head, part_rows)]
        outs += [made(SUB, part_rows, dtype=F32)]
    places, own, label, slot, *early = call(
        functools.partial(index_kernel, parts=parts, split=split, cap_groups=cap_groups),
        "index",
        outs,
        [ANY, VMEM, VMEM, ANY],
        [VMEM] * len(outs),
        scratch=[pltpu.VMEM(first_slots.shape, BF16), weight_scratch[0], pltpu.SemaphoreType.DMA((3,))],
        flops=full_flops // 4,
    )(got, parent, norm_gains, qkv_weight)
    send = call(
        functools.partial(second_kernel, parts=parts, split=split),
        "second",
        made(n_dev * cap_groups, width),
        [ANY] + [VMEM] * 4 + [ANY] * (len(early) + 4),
        scratch=[
            patch,
            patch,
            id_rows,
            qk,
            vt,
            *tile_scratch,
            *weight_scratch,
            pltpu.VMEM((rest_slots if split else first_slots).shape, BF16),
            pltpu.SemaphoreType.DMA((9,)),
        ],
        flops=full_flops,
    )(late if split else got, places, own, slot, norm_gains, *early, *weights)
    got = exchange(send.reshape(n_dev, cap_groups, width)).reshape(n_dev * cap_groups, width)
    return call(
        pool_kernel,
        "pool",
        made(groups, width, dtype=F32),
        [VMEM, VMEM],
    )(label, got)


def solution(mesh):
    placed = (P("vox", None), P("vox"), P("vox"), P("vox"), P(), P(), P(), P(), P())
    return jax.shard_map(
        shards, mesh=mesh, in_specs=placed, out_specs=P("vox", None), check_vma=False
    )
```

time: 191 us -> 185 us (0.969)
  blocking collectives: 118 us -> 14.4 us
  waiting for transfers between devices: 0.01 us -> 81.8 us
  starting transfers between devices: 2.81 us -> 17.7 us
    all_to_all x3 -> x1, blocking collectives: 118 us -> 14.4 us  [exchange(): return lax.all_to_all(data, 'vox', split_axis=0, concat_axis=0, tiled=True)]
    all_to_all x1 -> x3, waiting for transfers between devices: 0.01 us -> 81.8 us  [exchange(): return lax.all_to_all(data, 'vox', split_axis=0, concat_axis=0, tiled=True)]
    all_to_all x1 -> x3, starting transfers between devices: 2.81 us -> 17.7 us  [exchange(): return lax.all_to_all(data, 'vox', split_axis=0, concat_axis=0, tiled=True)]
    pallas_call x3 -> x5, Pallas kernels: 46.4 us -> 48.6 us  [the longest x1 23.9 us: shards(): call(functools.partial(second_kernel, parts=parts, split=split), 'second'...]
  transfers between devices with their start and end apart: 1 -> 3, of which waited for: 0 -> 2; matrix products, arithmetic and copies ran while one was open for 0% -> 0% of each run, Pallas kernels for 10% -> 12%
where the time goes in v1:
time: 185 us; the launch traced here: 184 us
  waiting for transfers between devices  81.8 us (44%)
  Pallas kernels  70 us (38%)
  starting transfers between devices  17.7 us (10%)
  blocking collectives  14.4 us (8%)
    all_to_all x3, waiting for transfers between devices, exchange(): return lax.all_to_all(data, 'vox', split_axis=0, concat_axis=0, tiled=True)  81.8 us
    pallas_call x1, Pallas kernels, shards(): call(functools.partial(second_kernel, parts=parts, split=split), 'second'...  23.9 us
    all_to_all x3, starting transfers between devices, exchange(): return lax.all_to_all(data, 'vox', split_axis=0, concat_axis=0, tiled=True)  17.7 us
    pallas_call x1, Pallas kernels, shards(): call(functools.partial(rest_kernel, parts=parts), 'rest', rest_slots, [AN...  17.1 us
    pallas_call x1, Pallas kernels, shards(): call(functools.partial(open_kernel, parts=parts, split=split), 'open', ou...  16 us
    all_to_all x1, blocking collectives, exchange(): return lax.all_to_all(data, 'vox', split_axis=0, concat_axis=0, tiled=True)  14.4 us
    pallas_call x1, Pallas kernels, shards(): call(functools.partial(pack_kernel, parts=parts), 'pack', slots(parts), [...  5.39 us
    pallas_call x1, Pallas kernels, shards(): call(functools.partial(index_kernel, parts=parts, split=split, cap_groups...  4.19 us
  transfers between devices with their start and end apart: 3, of which 2 were waited for; matrix products, arithmetic and copies ran while one was open for 0% of the time, Pallas kernels for 12%

profile of v1, /device:TPU:0, one launch (start us, length us, event | category | flops | bytes accessed | tf_op | source)
XLA Modules:
  0.0 184.1 jit_solution(2701117620823721761)
XLA Ops:
  0.0 5.4 %pack.1 = bf16[32,264,128]{2,1,0:T(8,128)(2,1)} custom-call(s32[1]{0:T(128)} %bitcast.me_ref, s32[1,1024]{1,0:T(1,128)} %bitcast.8, s32[1,1024]{1,0:T(1,128)} %bitcast.9, bf16[1024,512]{1,0:T(8,128)(2,1)} %x_hbm.1), custom_call_target="tpu_custom_call" | custom-call | tf_op jit(solution)/shard_map/pack/pallas_call | solution.py:603
  5.4 7.4 %all-to-all-start = ((bf16[32,264,128]{2,1,0:T(8,128)(2,1)}), bf16[32,264,128]{2,1,0:T(8,128)(2,1)}, u32[]{:S(2)}, u32[]{:S(2)}) async-start(bf16[32,264,128]{2,1,0:T(8,128)(2,1)} %pack.1), calls=%async_computation | async-start | bytes 4325376 | tf_op jit(solution)/shard_map/all_to_all | solution.py:560
  12.9 1.6 label.1.label_ref
  14.4 48.6 %all-to-all-done.got_hbm = bf16[32,264,128]{2,1,0:T(8,128)(2,1)} async-done(((bf16[32,264,128]{2,1,0:T(8,128)(2,1)}), bf16[32,264,128]{2,1,0:T(8,128)(2,1)}, u32[]{:S(2)}, u32[]{:S(2)}) %all-to-all-start) | async-done | bytes 2162720 | tf_op jit(solution)/shard_map/all_to_all | solution.py:560
  63.0 16.0 %open.1 = (bf16[32,72,128]{2,1,0:T(8,128)(2,1)}, bf16[1024,512]{1,0:T(8,128)(2,1)}, bf16[1024,1024]{1,0:T(8,128)(2,1)}, bf16[8,80,1024]{2,1,0:T(8,128)(2,1)}, s32[8,256]{1,0:T(8,128)}) custom-call(s32[1]{0:T(128)} %bitcast.me_ref, bf16[32,264,128]{2,1,0:T(8,128)(2,1)} %all-to-all-done.got_hbm, f32[8,512]{1,0:T(8,128)} %label.1.label_ref, ...), custom_call_target="tpu_custom_call" | custom-call | flops 4608000000 | bytes 15360000 | tf_op jit(solution)/shard_map/open/pallas_call | solution.py:630
  79.0 4.3 %all-to-all-start.1 = ((bf16[32,72,128]{2,1,0:T(8,128)(2,1)}), bf16[32,72,128]{2,1,0:T(8,128)(2,1)S(1)}, u32[]{:S(2)}, u32[]{:S(2)}) async-start(bf16[32,72,128]{2,1,0:T(8,128)(2,1)} %get-tuple-element.18), calls=%async_computation.1 | async-start | bytes 1179648 | tf_op jit(solution)/shard_map/all_to_all | solution.py:560
  83.3 17.1 %rest.1 = bf16[32,192,128]{2,1,0:T(8,128)(2,1)} custom-call(bf16[1024,512]{1,0:T(8,128)(2,1)} %get-tuple-element.20.x_hbm, bf16[1024,1024]{1,0:T(8,128)(2,1)} %get-tuple-element.21.qk_hbm, bf16[8,80,1024]{2,1,0:T(8,128)(2,1)} %get-tuple-element.22.vt_hbm, s32[8,256]{1,0:T(8,128)} %get-tuple-element.23.slot_ref, f32[2,2,512]{2,1,0:T(2,128)} %refs_4_.1, ...), custom_call_target="tpu_custom_call" | custom-call | flops 4608000000 | bytes 15360000 | tf_op jit(solution)/shard_map/rest/pallas_call | solution.py:653
  100.4 0.0 all-to-all-done.1.got_hbm
  100.4 0.0 copy-start
  100.4 6.0 %all-to-all-start.2 = ((bf16[32,192,128]{2,1,0:T(8,128)(2,1)}), bf16[32,192,128]{2,1,0:T(8,128)(2,1)}, u32[]{:S(2)}, u32[]{:S(2)}) async-start(bf16[32,192,128]{2,1,0:T(8,128)(2,1)} %rest.1), calls=%async_computation.2 | async-start | bytes 3145728 | tf_op jit(solution)/shard_map/all_to_all | solution.py:560
  106.4 0.0 copy-done
  106.4 4.2 %index.1 = (s32[8,512]{1,0:T(8,128)}, f32[8,512]{1,0:T(8,128)}, f32[8,256]{1,0:T(8,128)}, s32[8,128]{1,0:T(8,128)}, bf16[256,512]{1,0:T(8,128)(2,1)}, /*index=5*...) custom-call(bf16[32,72,128]{2,1,0:T(8,128)(2,1)} %copy-done, s32[1,128]{1,0:T(1,128)} %bitcast.11, ...), custom_call_target="tpu_custom_call" | custom-call | flops 2304000000 | bytes 7680000 | tf_op jit(solution)/shard_map/index/pallas_call | solution.py:680
  110.6 33.3 %all-to-all-done.2.refs_0_ = bf16[32,192,128]{2,1,0:T(8,128)(2,1)} async-done(((bf16[32,192,128]{2,1,0:T(8,128)(2,1)}), bf16[32,192,128]{2,1,0:T(8,128)(2,1)}, u32[]{:S(2)}, u32[]{:S(2)}) %all-to-all-start.2) | async-done | bytes 1572896 | tf_op jit(solution)/shard_map/all_to_all | solution.py:560
  143.9 23.9 %second.1 = bf16[256,512]{1,0:T(8,128)(2,1)} custom-call(bf16[32,192,128]{2,1,0:T(8,128)(2,1)} %all-to-all-done.2.refs_0_, s32[8,512]{1,0:T(8,128)} %get-tuple-element.24.refs_1_, f32[8,512]{1,0:T(8,128)} %get-tuple-element.25.refs_2_, s32[8,128]{1,0:T(8,128)} %get-tuple-element.26.refs_3_, f32[2,2,512]{2,1,0:T(2,128)} %refs_4_.1, ...), custom_call_target="tpu_custom_call" | custom-call | flops 9216000000 | bytes 30720000 | tf_op jit(solution)/shard_map/second/pallas_call | solution.py:689
  167.8 14.4 %all_to_all.20 = bf16[32,8,512]{2,1,0:T(8,128)(2,1)} all-to-all(bf16[32,8,512]{2,1,0:T(8,128)(2,1)} %bitcast.7), channel_id=1, replica_groups=mesh['vox'=32] {'vox'}, dimensions={0} | all-to-all | bytes 524288 | tf_op jit(solution)/shard_map/all_to_all | solution.py:560
  182.2 1.9 %pool.1 = f32[128,512]{1,0:T(8,128)} custom-call(f32[8,256]{1,0:T(8,128)} %get-tuple-element.19.label_ref, bf16[256,512]{1,0:T(8,128)(2,1)} %bitcast.6), custom_call_target="tpu_custom_call" | custom-call | tf_op jit(solution)/shard_map/pool/pallas_call | solution.py:708
Async XLA Ops:
  5.4 57.6 %all-to-all-start = ((bf16[32,264,128]{2,1,0:T(8,128)(2,1)}), bf16[32,264,128]{2,1,0:T(8,128)(2,1)}, u32[]{:S(2)}, u32[]{:S(2)}) async-start(bf16[32,264,128]{2,1,0:T(8,128)(2,1)} %pack.1), calls=%async_computation | async-start | bytes 4325376 | tf_op jit(solution)/shard_map/all_to_all | solution.py:560
  79.0 21.4 %all-to-all-start.1 = ((bf16[32,72,128]{2,1,0:T(8,128)(2,1)}), bf16[32,72,128]{2,1,0:T(8,128)(2,1)S(1)}, u32[]{:S(2)}, u32[]{:S(2)}) async-start(bf16[32,72,128]{2,1,0:T(8,128)(2,1)} %get-tuple-element.18), calls=%async_computation.1 | async-start | bytes 1179648 | tf_op jit(solution)/shard_map/all_to_all | solution.py:560
  100.4 6.0 %copy-start = (bf16[32,72,128]{2,1,0:T(8,128)(2,1)}, bf16[32,72,128]{2,1,0:T(8,128)(2,1)S(1)}, u32[]{:S(2)}) copy-start(bf16[32,72,128]{2,1,0:T(8,128)(2,1)S(1)} %all-to-all-done.1.got_hbm) | copy-start | bytes 1769476
  100.4 43.5 %all-to-all-start.2 = ((bf16[32,192,128]{2,1,0:T(8,128)(2,1)}), bf16[32,192,128]{2,1,0:T(8,128)(2,1)}, u32[]{:S(2)}, u32[]{:S(2)}) async-start(bf16[32,192,128]{2,1,0:T(8,128)(2,1)} %rest.1), calls=%async_computation.2 | async-start | bytes 3145728 | tf_op jit(solution)/shard_map/all_to_all | solution.py:560

commit v2 on v1

--- a/solution.py
+++ b/solution.py
@@ -225,6 +225,7 @@
     piece = up_w.shape[1] // pairs
     owner = iota((TILE, LANES), 1) // head
     cuts = [slice(at, at + TILE) for at in range(0, rows, TILE)]
+    alone = high == low + 1
 
     def masked_queries(t, pair):
         queries = qk_ref[tile_at(t), pair * LANES : (pair + 1) * LANES]
@@ -256,13 +257,18 @@
         after = (pair + 1) % pairs
         own = None if next_tile is None else masked_queries(next_tile, after)
         tops = [jnp.max(top, axis=0, keepdims=True) for top in tops]
-        next_tops, sums = None, None
+        next_tops, sums, probs = None, None, []
         for cut in cuts:
-            scores = None if own is None else score(own, after, cut)
-            probs = soften(pair, cut, tops)
+            scores = None if own is None or alone else score(own, after, cut)
+            probs.append(soften(pair, cut, tops))
             if own is not None:
+                scores = score(own, after, cut) if alone else scores
                 next_tops = keep(scores, after, cut, next_tops)
-            sums = mix(pair, cut, probs, sums)
+            if not alone:
+                sums = mix(pair, cut, probs[-1], sums)
+        if alone:
+            probs = [jnp.concatenate([p[j] for p in probs], axis=0) for j in range(per_pair)]
+            sums = mix(pair, slice(None), probs, None)
         for j in range(per_pair):
             h = pair * per_pair + j
             share = 1.0 / sums[j][head : head + SUB, :]
@@ -369,20 +375,23 @@
 
     gots[0].wait()
     ids = slot_ids(got_ref)
-    dest = jnp.concatenate([ids[2 * g : 2 * g + 1, :] for g in range(parts)], axis=1).astype(I32) - 1
-    parents = jnp.concatenate([ids[2 * g + 1 : 2 * g + 2, :] for g in range(parts)], axis=1) + 1.0
-    parents = jnp.broadcast_to(parents, (SUB, parents.shape[1])).astype(BF16)
+    packs = []
+    for g in range(parts):
+        both = ids[2 * g : 2 * g + 2, :] + iota((2, ids.shape[1]), 0).astype(F32)
+        packs.append((pack_places(both[0:1, :]), both))
+    gots[1].wait()
+    loads = start_all([(src.at[0], dst) for src, dst in zip(hbm, weights)], sems, 2)
+    for g, (places, both) in enumerate(packs):
+        both = jnp.concatenate([both] * (SUB // 2), axis=0)
+        receive_part(got_ref, g, places, both, slice(g * part_rows, (g + 1) * part_rows), y_ref, parents_ref)
+    dest = parents_ref[0:1, :].astype(I32) - 1
+    parents = jnp.broadcast_to(parents_ref[1:2, :], parents_ref.shape).astype(BF16)
     places, counts, starts = sort_places(dest, n_dev, rows, parts)
     slot_row = part_slots(counts, starts, part_rows, parts)
 
-    gots[1].wait()
-    loads = start_all([(src.at[0], dst) for src, dst in zip(hbm, weights)], sems, 2)
-
     def receive(t, carry):
         hot = one_hot(places - t * TILE == iota((TILE, places.shape[1]), 0))
-        for c in range(0, lanes_of, 2):
-            data = jnp.concatenate([slot_rows(got_ref, g, lanes_of, c, 2) for g in range(parts)], axis=0)
-            x_ref[tile_at(t), c * LANES : (c + 2) * LANES] = dot(hot, data).astype(BF16)
+        x_ref[tile_at(t), :] = dot(hot, y_ref[...]).astype(BF16)
         parents_ref[:, tile_at(t)] = dot(parents, hot, NT)
         return carry
 
@@ -444,6 +453,11 @@
         emit_rows(slot_ref[0:1, :], y_ref[g * part_rows : (g + 1) * part_rows, :], g - 1, send_ref)
 
 
+def pack_places(own):
+    ranks, _ = rank_rows(jnp.where(own > 0.0, 0, -1), SUB)
+    return jnp.concatenate([pick(hot, run) for hot, run in ranks], axis=1).astype(I32) - 1
+
+
 def receive_part(got_ref, group, places, own, at, x_ref, parents_ref):
     own = jnp.broadcast_to(own, (SUB, own.shape[1])).astype(BF16)
     lanes_of = x_ref.shape[1] // LANES
@@ -471,9 +485,7 @@
     slot_ref[...] = jnp.broadcast_to(group_slots(parent_ref[...], n_dev, cap_groups), slot_ref.shape)
     for g in range(parts):
         own = ids[g : g + 1, :]
-        ranks, _ = rank_rows(jnp.where(own > 0.0, 0, -1), SUB)
-        places = jnp.concatenate([pick(hot, run) for hot, run in ranks], axis=1).astype(I32) - 1
-        places_ref[g : g + 1, :] = places
+        places_ref[g : g + 1, :] = pack_places(own)
         own_ref[g : g + 1, :] = own
     gots[1].wait()
     wait_all(load)

time: 185 us -> 184 us (level)
  no operation moved by 1% of the time
where the time goes in v2:
time: 184 us
  waiting for transfers between devices  81.8 us (44%)
  Pallas kernels  69.5 us (38%)
  starting transfers between devices  17.7 us (10%)
  blocking collectives  14.4 us (8%)
    all_to_all x3, waiting for transfers between devices, exchange(): return lax.all_to_all(data, 'vox', split_axis=0, concat_axis=0, tiled=True)  81.8 us
    pallas_call x1, Pallas kernels, shards(): call(functools.partial(second_kernel, parts=parts, split=split), 'second'...  23.9 us
    all_to_all x3, starting transfers between devices, exchange(): return lax.all_to_all(data, 'vox', split_axis=0, concat_axis=0, tiled=True)  17.7 us
    pallas_call x1, Pallas kernels, shards(): call(functools.partial(rest_kernel, parts=parts), 'rest', rest_slots, [AN...  17.1 us
    pallas_call x1, Pallas kernels, shards(): call(functools.partial(open_kernel, parts=parts, split=split), 'open', ou...  15.5 us
    all_to_all x1, blocking collectives, exchange(): return lax.all_to_all(data, 'vox', split_axis=0, concat_axis=0, tiled=True)  14.4 us
    pallas_call x1, Pallas kernels, shards(): call(functools.partial(pack_kernel, parts=parts), 'pack', slots(parts), [...  5.39 us
    pallas_call x1, Pallas kernels, shards(): call(functools.partial(index_kernel, parts=parts, split=split, cap_groups...  4.19 us
  transfers between devices with their start and end apart: 3, of which 2 were waited for; matrix products, arithmetic and copies ran while one was open for 0% of the time, Pallas kernels for 12%

profile of v2, /device:TPU:0, one launch (start us, length us, event | category | flops | bytes accessed | tf_op | source)
XLA Modules:
  0.0 183.6 jit_solution(5837685333628754226)
XLA Ops:
  0.0 5.4 %pack.1 = bf16[32,264,128]{2,1,0:T(8,128)(2,1)} custom-call(s32[1]{0:T(128)} %bitcast.me_ref, s32[1,1024]{1,0:T(1,128)} %bitcast.8, s32[1,1024]{1,0:T(1,128)} %bitcast.9, bf16[1024,512]{1,0:T(8,128)(2,1)} %x_hbm.1), custom_call_target="tpu_custom_call" | custom-call | tf_op jit(solution)/shard_map/pack/pallas_call | solution.py:615
  5.4 7.4 %all-to-all-start = ((bf16[32,264,128]{2,1,0:T(8,128)(2,1)}), bf16[32,264,128]{2,1,0:T(8,128)(2,1)}, u32[]{:S(2)}, u32[]{:S(2)}) async-start(bf16[32,264,128]{2,1,0:T(8,128)(2,1)} %pack.1), calls=%async_computation | async-start | bytes 4325376 | tf_op jit(solution)/shard_map/all_to_all | solution.py:572
  12.9 1.6 label.1.label_ref
  14.4 48.6 %all-to-all-done.got_hbm = bf16[32,264,128]{2,1,0:T(8,128)(2,1)} async-done(((bf16[32,264,128]{2,1,0:T(8,128)(2,1)}), bf16[32,264,128]{2,1,0:T(8,128)(2,1)}, u32[]{:S(2)}, u32[]{:S(2)}) %all-to-all-start) | async-done | bytes 2162720 | tf_op jit(solution)/shard_map/all_to_all | solution.py:572
  63.0 15.5 %open.1 = (bf16[32,72,128]{2,1,0:T(8,128)(2,1)}, bf16[1024,512]{1,0:T(8,128)(2,1)}, bf16[1024,1024]{1,0:T(8,128)(2,1)}, bf16[8,80,1024]{2,1,0:T(8,128)(2,1)}, s32[8,256]{1,0:T(8,128)}) custom-call(s32[1]{0:T(128)} %bitcast.me_ref, bf16[32,264,128]{2,1,0:T(8,128)(2,1)} %all-to-all-done.got_hbm, f32[8,512]{1,0:T(8,128)} %label.1.label_ref, ...), custom_call_target="tpu_custom_call" | custom-call | flops 4608000000 | bytes 15360000 | tf_op jit(solution)/shard_map/open/pallas_call | solution.py:642
  78.5 4.3 %all-to-all-start.1 = ((bf16[32,72,128]{2,1,0:T(8,128)(2,1)}), bf16[32,72,128]{2,1,0:T(8,128)(2,1)S(1)}, u32[]{:S(2)}, u32[]{:S(2)}) async-start(bf16[32,72,128]{2,1,0:T(8,128)(2,1)} %get-tuple-element.18), calls=%async_computation.1 | async-start | bytes 1179648 | tf_op jit(solution)/shard_map/all_to_all | solution.py:572
  82.8 17.1 %rest.1 = bf16[32,192,128]{2,1,0:T(8,128)(2,1)} custom-call(bf16[1024,512]{1,0:T(8,128)(2,1)} %get-tuple-element.20.x_hbm, bf16[1024,1024]{1,0:T(8,128)(2,1)} %get-tuple-element.21.qk_hbm, bf16[8,80,1024]{2,1,0:T(8,128)(2,1)} %get-tuple-element.22.vt_hbm, s32[8,256]{1,0:T(8,128)} %get-tuple-element.23.slot_ref, f32[2,2,512]{2,1,0:T(2,128)} %refs_4_.1, ...), custom_call_target="tpu_custom_call" | custom-call | flops 4608000000 | bytes 15360000 | tf_op jit(solution)/shard_map/rest/pallas_call | solution.py:665
  99.9 0.0 all-to-all-done.1.got_hbm
  99.9 0.0 copy-start
  99.9 6.0 %all-to-all-start.2 = ((bf16[32,192,128]{2,1,0:T(8,128)(2,1)}), bf16[32,192,128]{2,1,0:T(8,128)(2,1)}, u32[]{:S(2)}, u32[]{:S(2)}) async-start(bf16[32,192,128]{2,1,0:T(8,128)(2,1)} %rest.1), calls=%async_computation.2 | async-start | bytes 3145728 | tf_op jit(solution)/shard_map/all_to_all | solution.py:572
  106.0 0.0 copy-done
  106.0 4.2 %index.1 = (s32[8,512]{1,0:T(8,128)}, f32[8,512]{1,0:T(8,128)}, f32[8,256]{1,0:T(8,128)}, s32[8,128]{1,0:T(8,128)}, bf16[256,512]{1,0:T(8,128)(2,1)}, /*index=5*...) custom-call(bf16[32,72,128]{2,1,0:T(8,128)(2,1)} %copy-done, s32[1,128]{1,0:T(1,128)} %bitcast.11, ...), custom_call_target="tpu_custom_call" | custom-call | flops 2304000000 | bytes 7680000 | tf_op jit(solution)/shard_map/index/pallas_call | solution.py:692
  110.2 33.3 %all-to-all-done.2.refs_0_ = bf16[32,192,128]{2,1,0:T(8,128)(2,1)} async-done(((bf16[32,192,128]{2,1,0:T(8,128)(2,1)}), bf16[32,192,128]{2,1,0:T(8,128)(2,1)}, u32[]{:S(2)}, u32[]{:S(2)}) %all-to-all-start.2) | async-done | bytes 1572896 | tf_op jit(solution)/shard_map/all_to_all | solution.py:572
  143.4 23.9 %second.1 = bf16[256,512]{1,0:T(8,128)(2,1)} custom-call(bf16[32,192,128]{2,1,0:T(8,128)(2,1)} %all-to-all-done.2.refs_0_, s32[8,512]{1,0:T(8,128)} %get-tuple-element.24.refs_1_, f32[8,512]{1,0:T(8,128)} %get-tuple-element.25.refs_2_, s32[8,128]{1,0:T(8,128)} %get-tuple-element.26.refs_3_, f32[2,2,512]{2,1,0:T(2,128)} %refs_4_.1, ...), custom_call_target="tpu_custom_call" | custom-call | flops 9216000000 | bytes 30720000 | tf_op jit(solution)/shard_map/second/pallas_call | solution.py:701
  167.3 14.4 %all_to_all.20 = bf16[32,8,512]{2,1,0:T(8,128)(2,1)} all-to-all(bf16[32,8,512]{2,1,0:T(8,128)(2,1)} %bitcast.7), channel_id=1, replica_groups=mesh['vox'=32] {'vox'}, dimensions={0} | all-to-all | bytes 524288 | tf_op jit(solution)/shard_map/all_to_all | solution.py:572
  181.7 1.9 %pool.1 = f32[128,512]{1,0:T(8,128)} custom-call(f32[8,256]{1,0:T(8,128)} %get-tuple-element.19.label_ref, bf16[256,512]{1,0:T(8,128)(2,1)} %bitcast.6), custom_call_target="tpu_custom_call" | custom-call | tf_op jit(solution)/shard_map/pool/pallas_call | solution.py:720
Async XLA Ops:
  5.4 57.6 %all-to-all-start = ((bf16[32,264,128]{2,1,0:T(8,128)(2,1)}), bf16[32,264,128]{2,1,0:T(8,128)(2,1)}, u32[]{:S(2)}, u32[]{:S(2)}) async-start(bf16[32,264,128]{2,1,0:T(8,128)(2,1)} %pack.1), calls=%async_computation | async-start | bytes 4325376 | tf_op jit(solution)/shard_map/all_to_all | solution.py:572
  78.5 21.4 %all-to-all-start.1 = ((bf16[32,72,128]{2,1,0:T(8,128)(2,1)}), bf16[32,72,128]{2,1,0:T(8,128)(2,1)S(1)}, u32[]{:S(2)}, u32[]{:S(2)}) async-start(bf16[32,72,128]{2,1,0:T(8,128)(2,1)} %get-tuple-element.18), calls=%async_computation.1 | async-start | bytes 1179648 | tf_op jit(solution)/shard_map/all_to_all | solution.py:572
  99.9 6.0 %copy-start = (bf16[32,72,128]{2,1,0:T(8,128)(2,1)}, bf16[32,72,128]{2,1,0:T(8,128)(2,1)S(1)}, u32[]{:S(2)}) copy-start(bf16[32,72,128]{2,1,0:T(8,128)(2,1)S(1)} %all-to-all-done.1.got_hbm) | copy-start | bytes 1769476
  99.9 43.5 %all-to-all-start.2 = ((bf16[32,192,128]{2,1,0:T(8,128)(2,1)}), bf16[32,192,128]{2,1,0:T(8,128)(2,1)}, u32[]{:S(2)}, u32[]{:S(2)}) async-start(bf16[32,192,128]{2,1,0:T(8,128)(2,1)} %rest.1), calls=%async_computation.2 | async-start | bytes 3145728 | tf_op jit(solution)/shard_map/all_to_all | solution.py:572
